TPU v7x, 512 devices: a whole 4x8x8 slice. The times are simulated.
512 devices in a mesh: dp: 2 (over core), ctx: 64 (over z, y), head: 4 (over x).
Axes of the slice: x: 4, y: 8, z: 8, core: 2. Of those that a mesh axis runs over, the one named last changes fastest.
Arguments:
- queries: bfloat16 [2, 8192, 2560], P('dp', 'ctx', 'head'), may hold values from -25 to 25
- keys: bfloat16 [2, 8192, 2560], P('dp', 'ctx', 'head'), may hold values from -25 to 25
- values: bfloat16 [2, 8192, 2560], P('dp', 'ctx', 'head'), may hold values from -6 to 6
- grad_y: bfloat16 [2, 8192, 2560], P('dp', 'ctx', 'head'), may hold values from -6 to 6
- out_gain: float32 [2560], P('head'), may hold values from 0.1 to 1.9
- offsets: int32 [2, 20], P(None, 'head'), may hold values from 0 to 63, as said below
Outputs:
- attended: bfloat16 [2, 8192, 2560], P('dp', 'ctx', 'head')
- query_grad: bfloat16 [2, 8192, 2560], P('dp', 'ctx', 'head')
- key_grad: bfloat16 [2, 8192, 2560], P('dp', 'ctx', 'head')
- value_grad: bfloat16 [2, 8192, 2560], P('dp', 'ctx', 'head')
- gain_grad: float32 [2560], P('head')
Inputs may be any that keep to these rules, and one draw needn't show every extreme that they name: Row 0 holds offsets below 8, row 1 offsets below 64.
All inputs are finite; a program needn't handle non-finite values.
Results may differ from a plain program's by a relative error of at most 0.011.
Values may be sent and summed in bfloat16 or wider, within the bound.
A program may use at most 64 MiB of HBM per device.

v0:
```python
import math
import jax
import jax.numpy as jnp
from jax import lax
from jax.sharding import PartitionSpec as P

HEAD_DIM = 128
SPAN = 4
R1 = 8
EPS = 1e-06


def swapped(block, axis, bit):
    count = lax.axis_size(axis)
    route = []
    for low in range(count):
        high = low | 1 << bit
        if high != low and high < count:
            route += [(low, high), (high, low)]
    return lax.ppermute(block, axis, route)


def pick_rows(source_rows, dilation, shifts):
    row_count, head_count, head_width = source_rows.shape
    grouped = source_rows.reshape(row_count // dilation, dilation, head_count, head_width)
    hit_mask = jnp.arange(dilation, dtype=jnp.int32).reshape(1, dilation, 1, 1) == shifts.reshape(
        1, 1, head_count, 1
    )
    chosen = jnp.where(hit_mask, grouped, jnp.zeros((), source_rows.dtype))
    return jnp.sum(chosen, axis=1, dtype=source_rows.dtype)


def place_rows(row_values, dilation, shifts):
    row_count, head_count, head_width = row_values.shape
    hit_mask = jnp.arange(dilation, dtype=jnp.int32).reshape(1, dilation, 1, 1) == shifts.reshape(
        1, 1, head_count, 1
    )
    spread = jnp.where(hit_mask, row_values[:, None], jnp.zeros((), row_values.dtype))
    return spread.reshape(row_count * dilation, head_count, head_width)


def level_scores(q_rows, k_rows):
    score_scale = 1.0 / math.sqrt(q_rows.shape[-1])
    return (
        jnp.einsum("qhe,khe->hqk", q_rows, k_rows, preferred_element_type=jnp.float32) * score_scale
    )


def attend(q_rows, k_rows, v_rows):
    scores = level_scores(q_rows, k_rows)
    row_max = jnp.max(scores, axis=-1, keepdims=True)
    log_total = row_max[..., 0] + jnp.log(jnp.sum(jnp.exp(scores - row_max), axis=-1))
    soft_rows = jnp.exp(scores - log_total[..., None]).astype(jnp.bfloat16)
    level_out = jnp.einsum("hqk,khe->qhe", soft_rows, v_rows, preferred_element_type=jnp.float32)
    return (level_out, log_total.T)


def score_grads(q_rows, k_rows, v_rows, log_total, grad_low, row_shift):
    score_scale = 1.0 / math.sqrt(q_rows.shape[-1])
    scores = level_scores(q_rows, k_rows)
    exact_soft = jnp.exp(scores - log_total.T[..., None])
    prob_grad = jnp.einsum("qhe,khe->hqk", grad_low, v_rows, preferred_element_type=jnp.float32)
    score_grad = (exact_soft * (prob_grad + row_shift.T[..., None]) * score_scale).astype(
        jnp.bfloat16
    )
    return (score_grad, exact_soft.astype(jnp.bfloat16))


def key_parts(score_grad, soft_low, q_rows, grad_low):
    k_part = jnp.einsum("hqk,qhe->khe", score_grad, q_rows, preferred_element_type=jnp.float32)
    v_part = jnp.einsum("hqk,qhe->khe", soft_low, grad_low, preferred_element_type=jnp.float32)
    return (k_part, v_part)


def query_part(score_grad, k_rows):
    return jnp.einsum("hqk,khe->qhe", score_grad, k_rows, preferred_element_type=jnp.float32)


def shards(queries, keys, values, grad_y, out_gain, offsets):
    tokens = queries.shape[1]
    flat_width = queries.shape[2]
    head_count = flat_width // HEAD_DIM
    row_shape = (tokens, head_count, HEAD_DIM)
    q_own = queries[0].reshape(row_shape)
    k_own = keys[0].reshape(row_shape)
    v_own = values[0].reshape(row_shape)
    ctx_size = lax.axis_size("ctx")
    span_bits = SPAN.bit_length() - 1
    my_place = lax.axis_index("ctx")
    mid_shift = offsets[0]
    top_shift = offsets[1]
    positions = jnp.arange(tokens, dtype=jnp.int32)
    mid_hit = (positions % R1)[:, None] == mid_shift[None, :]
    top_hit = (positions % ctx_size)[:, None] == top_shift[None, :]
    mid_q = pick_rows(q_own, R1, mid_shift)
    mid_k = pick_rows(k_own, R1, mid_shift)
    mid_v = pick_rows(v_own, R1, mid_shift)
    top_q = pick_rows(q_own, ctx_size, top_shift)
    top_k = pick_rows(k_own, ctx_size, top_shift)
    top_v = pick_rows(v_own, ctx_size, top_shift)
    mid_keys = mid_k.reshape(-1, flat_width)
    mid_vals = mid_v.reshape(-1, flat_width)
    top_keys = top_k.reshape(-1, flat_width)
    top_vals = top_v.reshape(-1, flat_width)

    def append_peer(mine, received, level_bit):
        upper_side = my_place >> level_bit & 1 == 1
        return jnp.where(
            upper_side, jnp.concatenate([received, mine], 0), jnp.concatenate([mine, received], 0)
        )

    for level_bit in range(span_bits):
        received = swapped((mid_keys, mid_vals), "ctx", level_bit)
        mid_keys = append_peer(mid_keys, received[0], level_bit)
        mid_vals = append_peer(mid_vals, received[1], level_bit)
    top_keys, top_vals = (
        lax.all_gather(top_keys, "ctx", axis=0, tiled=True),
        lax.all_gather(top_vals, "ctx", axis=0, tiled=True),
    )
    mid_keys = mid_keys.reshape(-1, head_count, HEAD_DIM)
    mid_vals = mid_vals.reshape(-1, head_count, HEAD_DIM)
    top_keys = top_keys.reshape(-1, head_count, HEAD_DIM)
    top_vals = top_vals.reshape(-1, head_count, HEAD_DIM)
    base_out, base_total = attend(q_own, k_own, v_own)
    mid_out, mid_total = attend(mid_q, mid_keys, mid_vals)
    top_out, top_total = attend(top_q, top_keys, top_vals)
    mid_full = place_rows(mid_total[..., None], R1, mid_shift)[..., 0]
    top_full = place_rows(top_total[..., None], ctx_size, top_shift)[..., 0]
    row_max = jnp.maximum(base_total, jnp.where(mid_hit, mid_full, base_total))
    row_max = jnp.maximum(row_max, jnp.where(top_hit, top_full, base_total))
    base_expo = jnp.exp(base_total - row_max)
    mid_expo = jnp.where(mid_hit, jnp.exp(mid_full - row_max), 0.0)
    top_expo = jnp.where(top_hit, jnp.exp(top_full - row_max), 0.0)
    denom = base_expo + mid_expo + top_expo
    base_share = base_expo / denom
    mid_share = mid_expo / denom
    top_share = top_expo / denom
    attn = (
        base_share[..., None] * base_out
        + mid_share[..., None] * place_rows(mid_out, R1, mid_shift)
        + top_share[..., None] * place_rows(top_out, ctx_size, top_shift)
    )
    inv_rms = lax.rsqrt(jnp.mean(attn * attn, axis=-1, keepdims=True) + EPS)
    normed = attn * inv_rms
    gain_rows = out_gain.reshape(head_count, HEAD_DIM)
    attended = (normed * gain_rows).astype(jnp.bfloat16).reshape(1, tokens, flat_width)
    grad_full = grad_y[0].reshape(row_shape).astype(jnp.float32)
    gain_part = jnp.sum(grad_full * normed, axis=0).reshape(flat_width)
    gain_grad = lax.psum(gain_part, ("dp", "ctx"))
    grad_norm = grad_full * gain_rows
    grad_attn = inv_rms * (
        grad_norm - normed * jnp.mean(grad_norm * normed, axis=-1, keepdims=True)
    )
    inner = jnp.sum(grad_attn * attn, axis=-1)
    base_low = (base_share[..., None] * grad_attn).astype(jnp.bfloat16)
    base_shift = -(base_share * inner)
    base_grad, base_soft = score_grads(q_own, k_own, v_own, base_total, base_low, base_shift)
    base_dq = query_part(base_grad, k_own)
    base_dk, base_dv = key_parts(base_grad, base_soft, q_own, base_low)
    mid_sel = pick_rows(mid_share[..., None], R1, mid_shift)[..., 0]
    mid_low = (mid_sel[..., None] * pick_rows(grad_attn, R1, mid_shift)).astype(jnp.bfloat16)
    mid_row_shift = -(mid_sel * pick_rows(inner[..., None], R1, mid_shift)[..., 0])
    mid_grad, mid_soft = score_grads(mid_q, mid_keys, mid_vals, mid_total, mid_low, mid_row_shift)
    mid_dq = query_part(mid_grad, mid_keys)
    mid_dk, mid_dv = key_parts(mid_grad, mid_soft, mid_q, mid_low)
    mid_dk = mid_dk.reshape(-1, flat_width)
    mid_dv = mid_dv.reshape(-1, flat_width)
    for level_bit in reversed(range(span_bits)):
        half_rows = mid_dk.shape[0] // 2
        upper_side = my_place >> level_bit & 1 == 1
        keep_k = jnp.where(upper_side, mid_dk[half_rows:], mid_dk[:half_rows])
        keep_v = jnp.where(upper_side, mid_dv[half_rows:], mid_dv[:half_rows])
        send_k = jnp.where(upper_side, mid_dk[:half_rows], mid_dk[half_rows:])
        send_v = jnp.where(upper_side, mid_dv[:half_rows], mid_dv[half_rows:])
        received = (
            swapped(send_k.astype(jnp.bfloat16), "ctx", level_bit).astype(send_k.dtype),
            swapped(send_v.astype(jnp.bfloat16), "ctx", level_bit).astype(send_v.dtype),
        )
        mid_dk = keep_k + received[0]
        mid_dv = keep_v + received[1]
    mid_dk = mid_dk.reshape(-1, head_count, HEAD_DIM)
    mid_dv = mid_dv.reshape(-1, head_count, HEAD_DIM)
    top_sel = pick_rows(top_share[..., None], ctx_size, top_shift)[..., 0]
    top_low = (top_sel[..., None] * pick_rows(grad_attn, ctx_size, top_shift)).astype(jnp.bfloat16)
    top_row_shift = -(top_sel * pick_rows(inner[..., None], ctx_size, top_shift)[..., 0])
    top_grad, top_soft = score_grads(top_q, top_keys, top_vals, top_total, top_low, top_row_shift)
    top_dq = query_part(top_grad, top_keys)
    gathered_dk, gathered_dv = key_parts(top_grad, top_soft, top_q, top_low)
    summed = (
        lax.psum_scatter(
            gathered_dk.reshape(-1, flat_width), "ctx", scatter_dimension=0, tiled=True
        ),
        lax.psum_scatter(
            gathered_dv.reshape(-1, flat_width), "ctx", scatter_dimension=0, tiled=True
        ),
    )
    top_dk = summed[0].reshape(-1, head_count, HEAD_DIM)
    top_dv = summed[1].reshape(-1, head_count, HEAD_DIM)
    query_grad = (
        base_dq + place_rows(mid_dq, R1, mid_shift) + place_rows(top_dq, ctx_size, top_shift)
    )
    key_grad = base_dk + place_rows(mid_dk, R1, mid_shift) + place_rows(top_dk, ctx_size, top_shift)
    value_grad = (
        base_dv + place_rows(mid_dv, R1, mid_shift) + place_rows(top_dv, ctx_size, top_shift)
    )
    out_shape = (1, tokens, flat_width)
    return (
        attended,
        query_grad.astype(jnp.bfloat16).reshape(out_shape),
        key_grad.astype(jnp.bfloat16).reshape(out_shape),
        value_grad.astype(jnp.bfloat16).reshape(out_shape),
        gain_grad,
    )


def solution(mesh):
    in_specs = (
        P("dp", "ctx", "head"),
        P("dp", "ctx", "head"),
        P("dp", "ctx", "head"),
        P("dp", "ctx", "head"),
        P("head"),
        P(None, "head"),
    )
    out_specs = (
        P("dp", "ctx", "head"),
        P("dp", "ctx", "head"),
        P("dp", "ctx", "head"),
        P("dp", "ctx", "head"),
        P("head"),
    )
    return jax.shard_map(shards, mesh=mesh, in_specs=in_specs, out_specs=out_specs, check_vma=False)
```

profile of v0, /device:TPU:266, one launch (start us, length us, event | category | flops | bytes accessed | tf_op | source)
XLA Modules:
  0.0 443.0 jit_solution(7934693849912801585)
XLA Ops:
  7.2 0.8 slice_bitcast_fusion.1
  8.0 1.5 fusion.26
  9.6 2.4 collective-permute-start
  12.0 3.6 collective-permute-start.2
  15.9 0.2 reshape_reshape_squeeze.20
  16.2 0.2 reshape_reshape_squeeze.21
  16.4 0.7 copy-done.2
  17.1 0.2 reshape_reshape_squeeze.23
  17.5 0.3 select_reduce_fusion
  17.8 48.5 %all-gather = bf16[64,2,640]{2,1,0:T(2,128)(2,1)S(1)} all-gather(bf16[1,2,640]{2,1,0:T(2,128)(2,1)S(1)} %reshape.367), channel_id=1, replica_groups=mesh['dp'=2,'ctx'=64,'head'=4] {'ctx'}, dimensions={0}, use_global_device_ids=true | all-gather | bytes 166400 | tf_op jit(solution)/shard_map/all_gather | solution.py:117
  66.4 0.3 fusion.58
  66.7 0.2 exponential_reduce_fusion.2
  67.0 47.4 %all-gather.1 = bf16[64,2,640]{2,1,0:T(2,128)(2,1)S(1)} all-gather(bf16[1,2,640]{2,1,0:T(2,128)(2,1)S(1)} %reshape.369), channel_id=1, replica_groups=mesh['dp'=2,'ctx'=64,'head'=4] {'ctx'}, dimensions={0}, use_global_device_ids=true | all-gather | bytes 166400 | tf_op jit(solution)/shard_map/all_gather | solution.py:118
  114.6 0.3 fusion.60
  115.4 0.5 copy-done.4
  116.4 1.3 dynamic-slice
  118.4 4.6 %collective-permute-start.1 = (bf16[32,640]{1,0:T(8,128)(2,1)S(1)}, bf16[32,640]{1,0:T(8,128)(2,1)S(1)}, u32[]{:S(2)}, u32[]{:S(2)}) collective-permute-start(bf16[32,640]{1,0:T(8,128)(2,1)S(1)} %maximum_select_fusion.2), channel_id=1, source_target_pairs={{0,8},{8,0},{4,12},{12,4},{16,24},{24,16},{20,28},{28,20},{32,40},... | collective-permute-start | bytes 122888 | tf_op jit(solution)/shard_map/ppermute | solution.py:20
  123.0 2.2 collective-permute-start.3
  125.3 0.2 fusion.59
  126.2 0.2 fusion.23
  126.4 3.4 collective-permute-done.3
  129.8 0.2 convolution_bitcast_fusion.7
  130.0 0.5 multiply_reduce_fusion.3
  130.6 0.7 copy-done.5
  131.2 0.3 multiply_reduce_fusion
  131.5 0.3 fusion.22
  132.1 0.2 fusion.21
  132.7 0.2 fusion.20
  133.0 1.0 fusion.50
  134.1 1.0 fusion.47
  135.1 0.4 fusion.14
  135.6 0.3 convolution_bitcast_fusion.4
  135.9 0.2 fusion.17
  136.1 2.2 collective-permute-start.6
  138.3 0.2 convolution_bitcast_fusion.5
  138.7 4.6 %collective-permute-start.4 = (bf16[32,640]{1,0:T(8,128)(2,1)S(1)}, bf16[32,640]{1,0:T(8,128)(2,1)S(1)}, u32[]{:S(2)}, u32[]{:S(2)}) collective-permute-start(bf16[32,640]{1,0:T(8,128)(2,1)S(1)} %copy_bitcast_fusion.1), channel_id=1, source_target_pairs={{0,8},{8,0},{4,12},{12,4},{16,24},{24,16},{20,28},{28,20},{32,40},... | collective-permute-start | bytes 122888 | tf_op jit(solution)/shard_map/ppermute | solution.py:20
  143.4 0.8 copy.198
  144.3 275.7 %psum.7 = f32[640]{0:T(1024)} all-reduce(f32[640]{0:T(1024)S(1)} %bitcast.253), channel_id=1, replica_groups=mesh['dp'=2,'ctx'=64,'head'=4] {'dp','ctx'}, use_global_device_ids=true, to_apply=%region_24.25 | all-reduce | flops 640 | bytes 5120 | tf_op jit(solution)/shard_map/psum | solution.py:149
  420.0 4.7 %collective-permute-start.7 = (bf16[16,640]{1,0:T(8,128)(2,1)S(1)}, bf16[16,640]{1,0:T(8,128)(2,1)S(1)}, u32[]{:S(2)}, u32[]{:S(2)}) collective-permute-start(bf16[16,640]{1,0:T(8,128)(2,1)S(1)} %select_convert_fusion.2), channel_id=1, source_target_pairs={{0,4},{4,0},{8,12},{12,8},{16,20},{20,16},{24,28},{28,24},{32,36},... | collective-permute-start | bytes 61448 | tf_op jit(solution)/shard_map/ppermute | solution.py:20
  424.8 1.9 collective-permute-start.5
  426.8 3.7 collective-permute-done.5
  430.6 1.2 constant_dynamic-slice_fusion.1
  432.4 0.2 fusion.12
  432.8 0.8 copy.200
  433.6 0.3 fusion.11
  434.1 0.8 copy.199
  434.9 0.3 fusion.13
  435.4 0.8 copy.201
  (89 shorter events, 5.4 us)
Async XLA Ops:
  7.2 423.4 %all-reduce.5.cloned.1.call-start = ((), (), s32[]{:S(2)}) async-start(), calls=%async_computation | async-start | bytes 1310720
  8.0 7.6 %copy-start = (bf16[1,128,640]{2,1,0:T(8,128)(2,1)S(1)}, bf16[1,128,640]{2,1,0:T(8,128)(2,1)}, u32[]{:S(2)}) copy-start(bf16[1,128,640]{2,1,0:T(8,128)(2,1)} %param.6) | copy-start | bytes 491524
  9.6 108.7 %collective-permute-start = (bf16[16,640]{1,0:T(8,128)(2,1)S(1)}, bf16[16,640]{1,0:T(8,128)(2,1)S(1)}, u32[]{:S(2)}, u32[]{:S(2)}) collective-permute-start(bf16[16,640]{1,0:T(8,128)(2,1)S(1)} %copy_bitcast_fusion.7), channel_id=1, source_target_pairs={{0,4},{4,0},{8,12},{12,8},{16,20},{20,16},{24,28},{28,24},{32,36},... | collective-permute-start | bytes 61448 | tf_op jit(solution)/shard_map/ppermute | solution.py:20
  12.0 3.8 copy-start.1
  12.0 106.4 %collective-permute-start.2 = (bf16[16,640]{1,0:T(8,128)(2,1)S(1)}, bf16[16,640]{1,0:T(8,128)(2,1)S(1)}, u32[]{:S(2)}, u32[]{:S(2)}) collective-permute-start(bf16[16,640]{1,0:T(8,128)(2,1)S(1)} %copy_bitcast_fusion.6), channel_id=1, source_target_pairs={{0,4},{4,0},{8,12},{12,8},{16,20},{20,16},{24,28},{28,24},{32,36},... | collective-permute-start | bytes 61448 | tf_op jit(solution)/shard_map/ppermute | solution.py:20
  16.2 0.9 copy-start.2
  115.0 0.9 copy-start.4
  118.4 6.9 %collective-permute-start.1 = (bf16[32,640]{1,0:T(8,128)(2,1)S(1)}, bf16[32,640]{1,0:T(8,128)(2,1)S(1)}, u32[]{:S(2)}, u32[]{:S(2)}) collective-permute-start(bf16[32,640]{1,0:T(8,128)(2,1)S(1)} %maximum_select_fusion.2), channel_id=1, source_target_pairs={{0,8},{8,0},{4,12},{12,4},{16,24},{24,16},{20,28},{28,20},{32,40},... | collective-permute-start | bytes 122888 | tf_op jit(solution)/shard_map/ppermute | solution.py:20
  123.0 6.8 %collective-permute-start.3 = (bf16[32,640]{1,0:T(8,128)(2,1)S(1)}, bf16[32,640]{1,0:T(8,128)(2,1)S(1)}, u32[]{:S(2)}, u32[]{:S(2)}) collective-permute-start(bf16[32,640]{1,0:T(8,128)(2,1)S(1)} %maximum_select_fusion.4), channel_id=1, source_target_pairs={{0,8},{8,0},{4,12},{12,4},{16,24},{24,16},{20,28},{28,20},{32,40},... | collective-permute-start | bytes 122888 | tf_op jit(solution)/shard_map/ppermute | solution.py:20
  130.5 0.7 copy-start.5
  136.1 283.9 %collective-permute-start.6 = (bf16[32,640]{1,0:T(8,128)(2,1)S(1)}, bf16[32,640]{1,0:T(8,128)(2,1)S(1)}, u32[]{:S(2)}, u32[]{:S(2)}) collective-permute-start(bf16[32,640]{1,0:T(8,128)(2,1)S(1)} %copy_bitcast_fusion), channel_id=1, source_target_pairs={{0,8},{8,0},{4,12},{12,4},{16,24},{24,16},{20,28},{28,20},{32,40},... | collective-permute-start | bytes 122888 | tf_op jit(solution)/shard_map/ppermute | solution.py:20
  138.7 286.1 %collective-permute-start.4 = (bf16[32,640]{1,0:T(8,128)(2,1)S(1)}, bf16[32,640]{1,0:T(8,128)(2,1)S(1)}, u32[]{:S(2)}, u32[]{:S(2)}) collective-permute-start(bf16[32,640]{1,0:T(8,128)(2,1)S(1)} %copy_bitcast_fusion.1), channel_id=1, source_target_pairs={{0,8},{8,0},{4,12},{12,4},{16,24},{24,16},{20,28},{28,20},{32,40},... | collective-permute-start | bytes 122888 | tf_op jit(solution)/shard_map/ppermute | solution.py:20
  420.0 6.7 %collective-permute-start.7 = (bf16[16,640]{1,0:T(8,128)(2,1)S(1)}, bf16[16,640]{1,0:T(8,128)(2,1)S(1)}, u32[]{:S(2)}, u32[]{:S(2)}) collective-permute-start(bf16[16,640]{1,0:T(8,128)(2,1)S(1)} %select_convert_fusion.2), channel_id=1, source_target_pairs={{0,4},{4,0},{8,12},{12,8},{16,20},{20,16},{24,28},{28,24},{32,36},... | collective-permute-start | bytes 61448 | tf_op jit(solution)/shard_map/ppermute | solution.py:20
  424.8 5.7 %collective-permute-start.5 = (bf16[16,640]{1,0:T(8,128)(2,1)S(1)}, bf16[16,640]{1,0:T(8,128)(2,1)S(1)}, u32[]{:S(2)}, u32[]{:S(2)}) collective-permute-start(bf16[16,640]{1,0:T(8,128)(2,1)S(1)} %select_convert_fusion.3), channel_id=1, source_target_pairs={{0,4},{4,0},{8,12},{12,8},{16,20},{20,16},{24,28},{28,24},{32,36},... | collective-permute-start | bytes 61448 | tf_op jit(solution)/shard_map/ppermute | solution.py:20
  430.6 1.2 copy-start.3
Sparse Core Ops, SparseCore 0:
  144.4 154.0 all-reduce.4
where the time goes:
time: 444 us; the launch traced here: 443 us
  blocking collectives  372 us (84%)
  starting transfers between devices  26.2 us (6%)
  between operations  15.2 us (3%)
  local copies, waits for them, and re-layouts  12.3 us (3%)
  waiting for transfers between devices  7.26 us (2%)
  matrix products  6.13 us (1%)
    psum x1, blocking collectives, shards(): gain_grad = lax.psum(gain_part, ('dp', 'ctx'))  276 us
    all_gather x1, blocking collectives, shards(): lax.all_gather(top_keys, 'ctx', axis=0, tiled=True)  48.5 us
    all_gather x1, blocking collectives, shards(): lax.all_gather(top_vals, 'ctx', axis=0, tiled=True)  47.4 us
    ppermute x8, starting transfers between devices, swapped(): return lax.ppermute(block, axis, route)  26.1 us
  transfers between devices with their start and end apart: 9, of which 3 were waited for; matrix products, arithmetic and copies ran while one was open for 2% of the time, Pallas kernels for 0%

commit v1 on v0

--- a/solution.py
+++ b/solution.py
@@ -146,7 +146,8 @@
     attended = (normed * gain_rows).astype(jnp.bfloat16).reshape(1, tokens, flat_width)
     grad_full = grad_y[0].reshape(row_shape).astype(jnp.float32)
     gain_part = jnp.sum(grad_full * normed, axis=0).reshape(flat_width)
-    gain_grad = lax.psum(gain_part, ("dp", "ctx"))
+    blocks = lax.all_gather(gain_part, ("dp", "ctx"))
+    gain_grad = jnp.sum(blocks, axis=0)
     grad_norm = grad_full * gain_rows
     grad_attn = inv_rms * (
         grad_norm - normed * jnp.mean(grad_norm * normed, axis=-1, keepdims=True)

time: 444 us -> 589 us (1.33)
  the two profiles are of different devices: /device:TPU:266 before, /device:TPU:2 now
where the time goes in v1:
time: 589 us
  blocking collectives  351 us (60%)
  waiting for transfers between devices  174 us (30%)
  starting transfers between devices  25.3 us (4%)
  between operations  15.2 us (3%)
  local copies, waits for them, and re-layouts  12.3 us (2%)
  matrix products  6.16 us (1%)
    all_gather x1, blocking collectives, shards(): blocks = lax.all_gather(gain_part, ('dp', 'ctx'))  247 us
    unnamed x2, waiting for transfers between devices  170 us
    all_gather x1, blocking collectives, shards(): lax.all_gather(top_keys, 'ctx', axis=0, tiled=True)  56.5 us
    all_gather x1, blocking collectives, shards(): lax.all_gather(top_vals, 'ctx', axis=0, tiled=True)  47.7 us
    ppermute x8, starting transfers between devices, swapped(): return lax.ppermute(block, axis, route)  25.3 us
  transfers between devices with their start and end apart: 9, of which 4 were waited for; matrix products, arithmetic and copies ran while one was open for 1% of the time, Pallas kernels for 0%

profile of v1, /device:TPU:2, one launch (start us, length us, event | category | flops | bytes accessed | tf_op | source)
XLA Modules:
  0.0 588.7 jit_solution(11819830100013709013)
XLA Ops:
  7.2 0.8 slice_bitcast_fusion.1
  8.0 1.5 fusion.26
  9.6 3.5 collective-permute-start
  13.1 2.5 collective-permute-start.2
  15.9 0.2 reshape_reshape_squeeze.20
  16.4 0.7 copy-done.2
  17.5 0.3 select_reduce_fusion
  17.8 56.5 %all-gather = bf16[64,2,640]{2,1,0:T(2,128)(2,1)S(1)} all-gather(bf16[1,2,640]{2,1,0:T(2,128)(2,1)S(1)} %reshape.363), channel_id=1, replica_groups=mesh['dp'=2,'ctx'=64,'head'=4] {'ctx'}, dimensions={0}, use_global_device_ids=true | all-gather | bytes 166400 | tf_op jit(solution)/shard_map/all_gather | solution.py:117
  74.4 0.3 fusion.58
  75.0 47.7 %all-gather.1 = bf16[64,2,640]{2,1,0:T(2,128)(2,1)S(1)} all-gather(bf16[1,2,640]{2,1,0:T(2,128)(2,1)S(1)} %reshape.365), channel_id=1, replica_groups=mesh['dp'=2,'ctx'=64,'head'=4] {'ctx'}, dimensions={0}, use_global_device_ids=true | all-gather | bytes 166400 | tf_op jit(solution)/shard_map/all_gather | solution.py:118
  122.9 0.3 fusion.60
  123.7 0.5 copy-done.4
  124.7 1.3 dynamic-slice
  126.7 2.7 collective-permute-start.1
  129.5 4.0 collective-permute-start.3
  133.5 0.5 collective-permute-done.1
  134.0 0.2 fusion.59
  134.8 0.2 fusion.23
  135.1 1.2 collective-permute-done.3
  136.3 0.2 convolution_bitcast_fusion.7
  136.5 0.5 multiply_reduce_fusion.3
  137.1 0.7 copy-done.5
  137.7 0.3 multiply_reduce_fusion
  138.0 0.3 fusion.22
  138.8 0.3 convolution_bitcast_fusion.4
  139.1 0.2 fusion.17
  139.4 0.2 convolution_bitcast_fusion.5
  139.7 0.3 fusion.21
  140.2 0.2 fusion.20
  140.6 1.0 fusion.50
  141.6 1.0 fusion.47
  142.6 0.4 fusion.14
  143.0 4.0 collective-permute-start.6
  147.0 2.7 collective-permute-start.4
  149.8 246.8 %all-gather.2 = f32[128,1,640]{2,1,0:T(1,128)S(1)} all-gather(f32[1,1,640]{2,1,0:T(1,128)S(1)} %reshape.367), channel_id=1, replica_groups=mesh['dp'=2,'ctx'=64,'head'=4] {'dp','ctx'}, dimensions={0}, use_global_device_ids=true | all-gather | bytes 330240 | tf_op jit(solution)/shard_map/all_gather | solution.py:149
  396.7 0.8 copy.198
  397.6 0.8 reduce_sum.199
  398.5 1.9 collective-permute-start.7
  400.4 3.9 collective-permute-start.5
  404.4 1.7 collective-permute-done.5
  406.1 170.2 %all-reduce.5.cloned.1.call-done = (f32[128,640]{0,1:T(8,128)}, f32[128,640]{0,1:T(8,128)}) async-done(((f32[128,640]{0,1:T(8,128)}, f32[128,640]{0,1:T(8,128)}), (f32[128,640]{0,1:T(8,128)}, f32[128,640]{0,1:T(8,128)})) %all-reduce.5.cloned.1.call-update) | async-done | bytes 655376
  576.3 1.2 constant_dynamic-slice_fusion.1
  578.1 0.2 fusion.12
  578.5 0.8 copy.200
  579.3 0.3 fusion.11
  579.8 0.8 copy.199
  580.6 0.3 fusion.13
  581.1 0.8 copy.201
  (91 shorter events, 5.8 us)
Async XLA Ops:
  7.2 569.1 %all-reduce.5.cloned.1.call-start = ((), (), s32[]{:S(2)}) async-start(), calls=%async_computation | async-start | bytes 1310720
  8.0 7.6 %copy-start = (bf16[1,128,640]{2,1,0:T(8,128)(2,1)S(1)}, bf16[1,128,640]{2,1,0:T(8,128)(2,1)}, u32[]{:S(2)}) copy-start(bf16[1,128,640]{2,1,0:T(8,128)(2,1)} %param.6) | copy-start | bytes 491524
  9.6 117.0 %collective-permute-start = (bf16[16,640]{1,0:T(8,128)(2,1)S(1)}, bf16[16,640]{1,0:T(8,128)(2,1)S(1)}, u32[]{:S(2)}, u32[]{:S(2)}) collective-permute-start(bf16[16,640]{1,0:T(8,128)(2,1)S(1)} %copy_bitcast_fusion.7), channel_id=1, source_target_pairs={{0,4},{4,0},{8,12},{12,8},{16,20},{20,16},{24,28},{28,24},{32,36},... | collective-permute-start | bytes 61448 | tf_op jit(solution)/shard_map/ppermute | solution.py:20
  13.1 2.7 copy-start.1
  13.1 113.6 %collective-permute-start.2 = (bf16[16,640]{1,0:T(8,128)(2,1)S(1)}, bf16[16,640]{1,0:T(8,128)(2,1)S(1)}, u32[]{:S(2)}, u32[]{:S(2)}) collective-permute-start(bf16[16,640]{1,0:T(8,128)(2,1)S(1)} %copy_bitcast_fusion.6), channel_id=1, source_target_pairs={{0,4},{4,0},{8,12},{12,8},{16,20},{20,16},{24,28},{28,24},{32,36},... | collective-permute-start | bytes 61448 | tf_op jit(solution)/shard_map/ppermute | solution.py:20
  16.2 0.9 copy-start.2
  123.3 0.9 copy-start.4
  126.7 7.2 %collective-permute-start.1 = (bf16[32,640]{1,0:T(8,128)(2,1)S(1)}, bf16[32,640]{1,0:T(8,128)(2,1)S(1)}, u32[]{:S(2)}, u32[]{:S(2)}) collective-permute-start(bf16[32,640]{1,0:T(8,128)(2,1)S(1)} %maximum_select_fusion.2), channel_id=1, source_target_pairs={{0,8},{8,0},{4,12},{12,4},{16,24},{24,16},{20,28},{28,20},{32,40},... | collective-permute-start | bytes 122888 | tf_op jit(solution)/shard_map/ppermute | solution.py:20
  129.5 6.8 %collective-permute-start.3 = (bf16[32,640]{1,0:T(8,128)(2,1)S(1)}, bf16[32,640]{1,0:T(8,128)(2,1)S(1)}, u32[]{:S(2)}, u32[]{:S(2)}) collective-permute-start(bf16[32,640]{1,0:T(8,128)(2,1)S(1)} %maximum_select_fusion.4), channel_id=1, source_target_pairs={{0,8},{8,0},{4,12},{12,4},{16,24},{24,16},{20,28},{28,20},{32,40},... | collective-permute-start | bytes 122888 | tf_op jit(solution)/shard_map/ppermute | solution.py:20
  137.0 0.7 copy-start.5
  143.0 255.4 %collective-permute-start.6 = (bf16[32,640]{1,0:T(8,128)(2,1)S(1)}, bf16[32,640]{1,0:T(8,128)(2,1)S(1)}, u32[]{:S(2)}, u32[]{:S(2)}) collective-permute-start(bf16[32,640]{1,0:T(8,128)(2,1)S(1)} %copy_bitcast_fusion), channel_id=1, source_target_pairs={{0,8},{8,0},{4,12},{12,4},{16,24},{24,16},{20,28},{28,20},{32,40},... | collective-permute-start | bytes 122888 | tf_op jit(solution)/shard_map/ppermute | solution.py:20
  147.0 253.3 %collective-permute-start.4 = (bf16[32,640]{1,0:T(8,128)(2,1)S(1)}, bf16[32,640]{1,0:T(8,128)(2,1)S(1)}, u32[]{:S(2)}, u32[]{:S(2)}) collective-permute-start(bf16[32,640]{1,0:T(8,128)(2,1)S(1)} %copy_bitcast_fusion.1), channel_id=1, source_target_pairs={{0,8},{8,0},{4,12},{12,4},{16,24},{24,16},{20,28},{28,20},{32,40},... | collective-permute-start | bytes 122888 | tf_op jit(solution)/shard_map/ppermute | solution.py:20
  398.5 5.9 %collective-permute-start.7 = (bf16[16,640]{1,0:T(8,128)(2,1)S(1)}, bf16[16,640]{1,0:T(8,128)(2,1)S(1)}, u32[]{:S(2)}, u32[]{:S(2)}) collective-permute-start(bf16[16,640]{1,0:T(8,128)(2,1)S(1)} %select_convert_fusion.2), channel_id=1, source_target_pairs={{0,4},{4,0},{8,12},{12,8},{16,20},{20,16},{24,28},{28,24},{32,36},... | collective-permute-start | bytes 61448 | tf_op jit(solution)/shard_map/ppermute | solution.py:20
  400.4 5.7 collective-permute-start.5
  576.3 1.2 copy-start.3
Sparse Core Ops, SparseCore 0:
  397.7 178.5 all-reduce.4
